TPU v7x, 512 devices: a whole 4x8x8 slice. The times are simulated.
512 devices in a mesh: row: 16 (over y_hi, z), col: 32 (over y_lo, x, core).
Axes of the slice: x: 4, y: 8 (y_hi: 2, y_lo: 4; y = y_hi * 4 + y_lo), z: 8, core: 2. Of those that a mesh axis runs over, the one named last changes fastest.
Arguments:
- features: bfloat16 [65536, 256], P(('col', 'row')), may hold values from -6 to 6
- weight: bfloat16 [256, 256], replicated, may hold values from -0.375 to 0.375
- bias: float32 [256], replicated, may hold values from -3 to 3
- grad_out: bfloat16 [65536, 256], P(('row', 'col')), may hold values from -6 to 6
- tile_rows: int32 [16, 32, 128], P('row', 'col'), may hold values from 0 to 31
- tile_cols: int32 [16, 32, 128], P('row', 'col'), may hold values from 0 to 15
- tile_counts: int32 [16, 32], P('row', 'col'), may hold values from 1 to 128, as said below
- tile_values: bfloat16 [16, 32, 128, 128, 128], P('row', 'col'), may hold values from 0 to 0.011962891
Outputs:
- output: bfloat16 [65536, 256], P(('row', 'col'))
- grad_features: bfloat16 [65536, 256], P(('col', 'row'))
- grad_weight: float32 [256, 256], replicated
- grad_bias: float32 [256], replicated
Inputs may be any that keep to these rules, and one draw needn't show every extreme that they name: `tile_counts`: some grid cell has all 128 slots live. Tile coordinates may repeat within a cell; repeated tiles add.
All inputs are finite; a program needn't handle non-finite values.
Results may differ from a plain program's by a relative error of at most 0.018.
Values may be sent and summed in bfloat16 or wider, within the bound.
No kernel may reach another device: no remote copies, remote signals or barrier semaphores. Data moves between devices by JAX's collectives and lax.ppermute only.
A program may use at most 64 MiB of HBM per device.

v0:
```python
import jax
import jax.numpy as jnp
from jax import lax
from jax.sharding import PartitionSpec as P

GROUP = 8


def elu_value(pre):
    return jnp.where(pre > 0, pre, jnp.expm1(jnp.minimum(pre, 0.0)))


def elu_slope(pre):
    return jnp.where(pre > 0, jnp.float32(1.0), jnp.exp(jnp.minimum(pre, 0.0)))


def accumulate(values, dest_idx, src_idx, live, source, dest_tiles, transpose):
    side = values.shape[-1]
    width = source.shape[-1]
    group_size = GROUP
    blocks_all = source.reshape(source.shape[0] // side, side, width)

    def one_group(step, acc):
        first = step * group_size
        part_values = lax.dynamic_slice_in_dim(values, first, group_size, 0)
        part_dest = lax.dynamic_slice_in_dim(dest_idx, first, group_size, 0)
        part_src = lax.dynamic_slice_in_dim(src_idx, first, group_size, 0)
        blocks = jnp.take(blocks_all, part_src, axis=0)
        if transpose:
            prod = jnp.einsum(
                "gab,gac->gbc", part_values, blocks, preferred_element_type=jnp.float32
            )
        else:
            prod = jnp.einsum(
                "gab,gbc->gac", part_values, blocks, preferred_element_type=jnp.float32
            )
        keep = (jnp.arange(group_size) + first < live).astype(jnp.float32)
        return acc.at[part_dest].add(prod * keep[:, None, None])

    start_acc = jnp.zeros((dest_tiles, side, width), jnp.float32)
    steps_used = values.shape[0] // group_size
    total = lax.fori_loop(0, steps_used, one_group, start_acc)
    return total.reshape(dest_tiles * side, width)


def body(features, weight, bias, grad_out, tile_rows, tile_cols, tile_counts, tile_values):
    values = tile_values[0, 0]
    rows_idx = tile_rows[0, 0]
    cols_idx = tile_cols[0, 0]
    live = tile_counts[0, 0]
    side = values.shape[-1]
    share = features.shape[0]
    row_tiles = share * lax.axis_size("col") // side
    col_tiles = share * lax.axis_size("row") // side
    mixed = jnp.dot(features, weight, preferred_element_type=jnp.float32).astype(jnp.bfloat16)
    column_block = lax.all_gather(mixed, "row", axis=0, tiled=True)
    partial_value = accumulate(values, rows_idx, cols_idx, live, column_block, row_tiles, False)
    pre_share = (
        lax.psum_scatter(
            partial_value.astype(jnp.bfloat16), "col", scatter_dimension=0, tiled=True
        ).astype(jnp.float32)
        + bias[None, :]
    )
    grad_share = (grad_out.astype(jnp.float32) * elu_slope(pre_share)).astype(jnp.bfloat16)
    grad_block = lax.all_gather(grad_share, "col", axis=0, tiled=True)
    output = elu_value(pre_share).astype(jnp.bfloat16)
    back = accumulate(values, cols_idx, rows_idx, live, grad_block, col_tiles, True)
    grad_mixed = lax.psum_scatter(back.astype(jnp.bfloat16), "row", scatter_dimension=0, tiled=True)
    grad_features = lax.dot_general(
        grad_mixed, weight, (((1,), (1,)), ((), ())), preferred_element_type=jnp.float32
    ).astype(jnp.bfloat16)
    weight_term = lax.dot_general(
        features, grad_mixed, (((0,), (0,)), ((), ())), preferred_element_type=jnp.float32
    )
    bias_term = jnp.sum(grad_share.astype(jnp.float32), axis=0)
    grad_weight, grad_bias = lax.psum((weight_term, bias_term), ("row", "col"))
    return (output, grad_features, grad_weight, grad_bias)


def solution(mesh):
    placed = (
        P(("col", "row"), None),
        P(),
        P(),
        P(("row", "col"), None),
        P("row", "col", None),
        P("row", "col", None),
        P("row", "col"),
        P("row", "col", None, None, None),
    )
    return jax.shard_map(
        body,
        mesh=mesh,
        in_specs=placed,
        out_specs=(P(("row", "col"), None), P(("col", "row"), None), P(), P()),
        check_vma=False,
    )
```

profile of v0, /device:TPU:23, one launch (start us, length us, event | category | flops | bytes accessed | tf_op | source)
XLA Modules:
  0.0 1037.7 jit_solution(1046019565683276147)
XLA Ops:
  9.8 93.5 %all-gather.3.cloned.1.call-done = bf16[2048,256]{1,0:T(8,128)(2,1)} async-done(((bf16[128,256]{1,0:T(8,128)(2,1)}), bf16[2048,256]{1,0:T(8,128)(2,1)}) %all-gather.3.cloned.1.call-update) | async-done | bytes 1048592 | tf_op jit(solution)/shard_map/all_gather | solution.py:56
  103.3 2.4 broadcast_in_dim.79
  105.7 96.6 %while.26 = (s32[]{:T(128)}, f32[32,128,256]{2,1,0:T(8,128)}, s32[128]{0:T(128)S(1)}, bf16[128,128,128]{2,1,0:T(8,128)(2,1)}, s32[128]{0:T(128)S(1)}, /*index=5*...) while((s32[]{:T(128)}, f32[32,128,256]{2,1,0:T(8,128)}, ...), condition=%wide.region_2.3_spmd, body=%wide.region_0.2_spmd.sunk | while | flops 67896424 | bytes 6033887 | solution.py:42
  108.4 3.3 scatter_fusion
  114.5 3.3 scatter_fusion
  120.6 3.3 scatter_fusion
  126.6 3.3 scatter_fusion
  132.7 3.2 scatter_fusion
  138.6 3.3 scatter_fusion
  144.6 3.3 scatter_fusion
  150.6 3.3 scatter_fusion
  156.7 3.2 scatter_fusion
  162.7 3.3 scatter_fusion
  168.7 3.3 scatter_fusion
  174.7 3.3 scatter_fusion
  180.8 3.3 scatter_fusion
  186.8 3.4 scatter_fusion
  192.9 3.4 scatter_fusion
  199.0 3.3 scatter_fusion
  202.3 3.8 convert_element_type.56
  206.2 125.6 %reduce-scatter.3.cloned.1.call-done = bf16[128,256]{1,0:T(8,128)(2,1)} async-done(((bf16[4096,256]{1,0:T(8,128)(2,1)}), bf16[128,256]{1,0:T(8,128)(2,1)}) %reduce-scatter.3.cloned.1.call-update) | async-done | bytes 65552 | tf_op jit(solution)/shard_map/reduce_scatter | solution.py:59
  333.5 6.4 copy.12
  339.9 75.5 %all-gather.5.cloned.1.call-done = bf16[4096,256]{1,0:T(8,128)(2,1)} async-done(((bf16[128,256]{1,0:T(8,128)(2,1)}), bf16[4096,256]{1,0:T(8,128)(2,1)}) %all-gather.5.cloned.1.call-update) | async-done | bytes 2097168 | tf_op jit(solution)/shard_map/all_gather | solution.py:65
  417.0 121.8 %while.27 = (s32[]{:T(128)}, f32[16,128,256]{2,1,0:T(8,128)}, s32[128]{0:T(128)S(1)}, bf16[128,128,128]{1,2,0:T(8,128)(2,1)}, s32[128]{0:T(128)S(1)}, /*index=5*...) while((s32[]{:T(128)}, f32[16,128,256]{2,1,0:T(8,128)}, ...), condition=%wide.region_6.7_spmd, body=%wide.region_4.6_spmd.sunk | while | flops 67896424 | bytes 6033887 | solution.py:42
  417.7 2.2 gather_fusion.1
  421.3 3.3 scatter_fusion.1
  425.3 2.2 gather_fusion.1
  428.9 3.3 scatter_fusion.1
  433.0 2.2 gather_fusion.1
  436.6 3.3 scatter_fusion.1
  440.6 2.2 gather_fusion.1
  444.2 3.3 scatter_fusion.1
  451.9 3.3 scatter_fusion.1
  459.4 3.3 scatter_fusion.1
  467.0 3.3 scatter_fusion.1
  474.6 3.3 scatter_fusion.1
  482.3 3.3 scatter_fusion.1
  489.9 3.3 scatter_fusion.1
  497.5 3.3 scatter_fusion.1
  505.1 3.3 scatter_fusion.1
  512.7 3.3 scatter_fusion.1
  520.3 3.3 scatter_fusion.1
  527.9 3.3 scatter_fusion.1
  535.6 3.3 scatter_fusion.1
  538.8 2.7 convert_element_type.62
  541.6 97.9 %psum.15 = f32[256]{0:T(256)} all-reduce(f32[256]{0:T(256)S(1)} %get-tuple-element.297), channel_id=1, replica_groups=mesh['row'=16,'col'=32] {'row','col'}, use_global_device_ids=true, to_apply=%region_10.11 | all-reduce | flops 256 | bytes 2048 | tf_op jit(solution)/shard_map/psum | solution.py:76
  639.5 113.2 %reduce-scatter.5.cloned.1.call-done = bf16[128,256]{1,0:T(8,128)(2,1)} async-done(((bf16[2048,256]{1,0:T(8,128)(2,1)}), bf16[128,256]{1,0:T(8,128)(2,1)}) %reduce-scatter.5.cloned.1.call-update) | async-done | bytes 65552 | tf_op jit(solution)/shard_map/reduce_scatter | solution.py:68
  756.2 273.2 %all-reduce.2.cloned.1.call-done = f32[256,256]{0,1:T(8,128)} async-done(((f32[256,256]{0,1:T(8,128)}), f32[256,256]{0,1:T(8,128)}) %all-reduce.2.cloned.1.call-update) | async-done | bytes 262160 | tf_op jit(solution)/shard_map/psum | solution.py:76
  (186 shorter events, 114.7 us)
Async XLA Ops:
  7.2 0.9 copy-start
  7.2 98.5 %copy-start.4 = (s32[1,1,128]{2,1,0:T(1,128)S(1)}, s32[1,1,128]{2,1,0:T(1,128)}, u32[]{:S(2)}) copy-start(s32[1,1,128]{2,1,0:T(1,128)} %param.16) | copy-start | bytes 1540
  7.2 98.5 %copy-start.5 = (s32[1,1,128]{2,1,0:T(1,128)S(1)}, s32[1,1,128]{2,1,0:T(1,128)}, u32[]{:S(2)}) copy-start(s32[1,1,128]{2,1,0:T(1,128)} %param.17) | copy-start | bytes 1540
  7.2 96.1 %all-gather.3.cloned.1.call-start = ((), (), s32[]{:S(2)}) async-start(), calls=%async_computation.2 | async-start | bytes 1114112 | tf_op jit(solution)/shard_map/all_gather | solution.py:56
  9.7 322.1 %reduce-scatter.3.cloned.1.call-start = ((), (), s32[]{:S(2)}) async-start(), calls=%async_computation.3 | async-start | bytes 2162688 | tf_op jit(solution)/shard_map/reduce_scatter | solution.py:59
  103.3 2.4 copy-start.1
  202.3 129.6 %copy-start.3 = (bf16[128,256]{1,0:T(8,128)(2,1)S(1)}, bf16[128,256]{1,0:T(8,128)(2,1)}, u32[]{:S(2)}) copy-start(bf16[128,256]{1,0:T(8,128)(2,1)} %param.15) | copy-start | bytes 196612
  202.3 129.6 %copy-start.6 = (f32[256]{0:T(256)S(1)}, f32[256]{0:T(256)}, u32[]{:S(2)}) copy-start(f32[256]{0:T(256)} %param.14) | copy-start | bytes 3076
  206.1 209.3 %all-gather.5.cloned.1.call-start = ((), (), s32[]{:S(2)}) async-start(), calls=%async_computation.4 | async-start | bytes 2162688 | tf_op jit(solution)/shard_map/all_gather | solution.py:65
  333.4 419.3 %reduce-scatter.5.cloned.1.call-start = ((), (), s32[]{:S(2)}) async-start(), calls=%async_computation.5 | async-start | bytes 1114112 | tf_op jit(solution)/shard_map/reduce_scatter | solution.py:68
  538.8 213.9 %copy-start.2 = (bf16[128,256]{1,0:T(8,128)(2,1)S(1)}, bf16[128,256]{1,0:T(8,128)(2,1)}, u32[]{:S(2)}) copy-start(bf16[128,256]{1,0:T(8,128)(2,1)} %param.12) | copy-start | bytes 196612
  541.6 487.8 %all-reduce.2.cloned.1.call-start = ((), (), s32[]{:S(2)}) async-start(), calls=%async_computation.6 | async-start | bytes 524288 | tf_op jit(solution)/shard_map/psum | solution.py:76
Sparse Core Ops, SparseCore 0:
  11.8 91.4 all-gather.2
  206.3 125.5 reduce-scatter.2
  334.8 80.5 all-gather.4
  541.7 210.9 reduce-scatter.4
  758.9 270.4 all-reduce.1
where the time goes:
time: 1040 us
  waiting for transfers between devices  681 us (65%)
  other arithmetic  140 us (13%)
  blocking collectives  97.9 us (9%)
  local copies, waits for them, and re-layouts  57 us (5%)
  matrix products  47.3 us (5%)
  between operations  13.8 us (1%)
    psum x1, waiting for transfers between devices, body(): grad_weight, grad_bias = lax.psum((weight_term, bias_term), ('row', 'col'))  273 us
    reduce_scatter x1, waiting for transfers between devices, body(): lax.psum_scatter(partial_value.astype(jnp.bfloat16), 'col', scatter_dimen...  126 us
    reduce_scatter x1, waiting for transfers between devices, body(): lax.psum_scatter(back.astype(jnp.bfloat16), 'row', scatter_dimension=0, t...  113 us
    scatter-add x32, other arithmetic, one_group(): return acc.at[part_dest].add(prod * keep[:, None, None])  106 us
    psum x1, blocking collectives, body(): grad_weight, grad_bias = lax.psum((weight_term, bias_term), ('row', 'col'))  97.9 us
    all_gather x1, waiting for transfers between devices, body(): column_block = lax.all_gather(mixed, 'row', axis=0, tiled=True)  93.5 us
    all_gather x1, waiting for transfers between devices, body(): grad_block = lax.all_gather(grad_share, 'col', axis=0, tiled=True)  75.5 us
    gather x32, local copies, waits for them, and re-layouts, one_group(): blocks = jnp.take(blocks_all, part_src, axis=0)  44 us
  transfers between devices with their start and end apart: 5, of which 5 were waited for; matrix products, arithmetic and copies ran while one was open for 1% of the time, Pallas kernels for 0%

commit v1 on v0

--- a/solution.py
+++ b/solution.py
@@ -1,9 +1,26 @@
+import functools
 import jax
 import jax.numpy as jnp
 from jax import lax
 from jax.sharding import PartitionSpec as P
 
 GROUP = 8
+
+
+def mix_layers_all_on(s0, along_axis):
+    block_next = jnp.concatenate(
+        lax.all_to_all(
+            jnp.stack(lax.axis_size(along_axis) * [s0], axis=0),
+            along_axis,
+            split_axis=0,
+            concat_axis=0,
+        ),
+        axis=0,
+    )
+    return block_next
+
+
+expand_the_rings = functools.partial(mix_layers_all_on, along_axis="row")
 
 
 def elu_value(pre):
@@ -53,7 +70,7 @@
     row_tiles = share * lax.axis_size("col") // side
     col_tiles = share * lax.axis_size("row") // side
     mixed = jnp.dot(features, weight, preferred_element_type=jnp.float32).astype(jnp.bfloat16)
-    column_block = lax.all_gather(mixed, "row", axis=0, tiled=True)
+    column_block = expand_the_rings(mixed)
     partial_value = accumulate(values, rows_idx, cols_idx, live, column_block, row_tiles, False)
     pre_share = (
         lax.psum_scatter(

time: 1040 us -> 993 us (0.955)
  waiting for transfers between devices: 681 us -> 619 us
  starting transfers between devices: 0.21 us -> 13.8 us
    all_gather x1 -> x0, waiting for transfers between devices: 93.5 us -> none  [body(): column_block = lax.all_gather(mixed, 'row', axis=0, tiled=True)]
    all_to_all x0 -> x1, waiting for transfers between devices: none -> 30.6 us  [mix_layers_all_on(): lax.all_to_all(jnp.stack(lax.axis_size(along_axis) * [s0], axis=0), along...]
    all_to_all x0 -> x1, starting transfers between devices: none -> 13.6 us  [mix_layers_all_on(): lax.all_to_all(jnp.stack(lax.axis_size(along_axis) * [s0], axis=0), along...]
where the time goes in v1:
time: 993 us; the launch traced here: 989 us
  waiting for transfers between devices  619 us (62%)
  other arithmetic  140 us (14%)
  blocking collectives  97.8 us (10%)
  local copies, waits for them, and re-layouts  58.1 us (6%)
  matrix products  46.7 us (5%)
  starting transfers between devices  13.8 us (1%)
  between operations  13.8 us (1%)
    psum x1, waiting for transfers between devices, body(): grad_weight, grad_bias = lax.psum((weight_term, bias_term), ('row', 'col'))  273 us
    reduce_scatter x1, waiting for transfers between devices, body(): lax.psum_scatter(partial_value.astype(jnp.bfloat16), 'col', scatter_dimen...  127 us
    reduce_scatter x1, waiting for transfers between devices, body(): lax.psum_scatter(back.astype(jnp.bfloat16), 'row', scatter_dimension=0, t...  113 us
    scatter-add x32, other arithmetic, one_group(): return acc.at[part_dest].add(prod * keep[:, None, None])  105 us
    psum x1, blocking collectives, body(): grad_weight, grad_bias = lax.psum((weight_term, bias_term), ('row', 'col'))  97.8 us
    all_gather x1, waiting for transfers between devices, body(): grad_block = lax.all_gather(grad_share, 'col', axis=0, tiled=True)  75.5 us
    gather x32, local copies, waits for them, and re-layouts, one_group(): blocks = jnp.take(blocks_all, part_src, axis=0)  44 us
    all_to_all x1, waiting for transfers between devices, mix_layers_all_on(): lax.all_to_all(jnp.stack(lax.axis_size(along_axis) * [s0], axis=0), along...  30.6 us
  transfers between devices with their start and end apart: 5, of which 5 were waited for; matrix products, arithmetic and copies ran while one was open for 1% of the time, Pallas kernels for 0%

profile of v1, /device:TPU:23, one launch (start us, length us, event | category | flops | bytes accessed | tf_op | source)
XLA Modules:
  0.0 989.4 jit_solution(15930878396133804536)
XLA Ops:
  10.2 13.6 %all-to-all-start = ((bf16[16,128,256]{2,1,0:T(8,128)(2,1)}), bf16[16,128,256]{2,1,0:T(8,128)(2,1)S(1)}, u32[]{:S(2)}, u32[]{:S(2)}) async-start(bf16[16,128,256]{2,1,0:T(8,128)(2,1)} %stack.2), calls=%async_computation | async-start | bytes 2097152 | tf_op jit(solution)/shard_map/all_to_all | solution.py:12
  23.8 30.6 %all-to-all-done = bf16[16,128,256]{2,1,0:T(8,128)(2,1)S(1)} async-done(((bf16[16,128,256]{2,1,0:T(8,128)(2,1)}), bf16[16,128,256]{2,1,0:T(8,128)(2,1)S(1)}, u32[]{:S(2)}, u32[]{:S(2)}) %all-to-all-start) | async-done | bytes 1048608 | tf_op jit(solution)/shard_map/all_to_all | solution.py:12
  54.4 2.4 broadcast_in_dim.79
  56.8 96.4 %while.26 = (s32[]{:T(128)}, f32[32,128,256]{2,1,0:T(8,128)}, s32[128]{0:T(128)S(1)}, bf16[128,128,128]{2,1,0:T(8,128)(2,1)}, s32[128]{0:T(128)S(1)}, /*index=5*...) while((s32[]{:T(128)}, f32[32,128,256]{2,1,0:T(8,128)}, ...), condition=%wide.region_2.3_spmd, body=%wide.region_0.2_spmd.sunk | while | flops 67896424 | bytes 6033887 | solution.py:59
  59.5 3.3 scatter_fusion
  65.5 3.4 scatter_fusion
  71.6 3.3 scatter_fusion
  77.7 3.3 scatter_fusion
  83.7 3.2 scatter_fusion
  89.7 3.3 scatter_fusion
  95.7 3.3 scatter_fusion
  101.7 3.3 scatter_fusion
  107.7 3.3 scatter_fusion
  113.7 3.3 scatter_fusion
  119.8 3.3 scatter_fusion
  125.8 3.4 scatter_fusion
  131.9 3.2 scatter_fusion
  137.9 3.3 scatter_fusion
  143.9 3.3 scatter_fusion
  149.9 3.3 scatter_fusion
  153.2 3.8 convert_element_type.56
  157.2 126.7 %reduce-scatter.3.cloned.1.call-done = bf16[128,256]{1,0:T(8,128)(2,1)} async-done(((bf16[4096,256]{1,0:T(8,128)(2,1)}), bf16[128,256]{1,0:T(8,128)(2,1)}) %reduce-scatter.3.cloned.1.call-update) | async-done | bytes 65552 | tf_op jit(solution)/shard_map/reduce_scatter | solution.py:76
  285.5 6.4 copy.12
  291.8 75.5 %all-gather.2.cloned.1.call-done = bf16[4096,256]{1,0:T(8,128)(2,1)} async-done(((bf16[128,256]{1,0:T(8,128)(2,1)}), bf16[4096,256]{1,0:T(8,128)(2,1)}) %all-gather.2.cloned.1.call-update) | async-done | bytes 2097168 | tf_op jit(solution)/shard_map/all_gather | solution.py:82
  368.9 121.9 %while.27 = (s32[]{:T(128)}, f32[16,128,256]{2,1,0:T(8,128)}, s32[128]{0:T(128)S(1)}, bf16[128,128,128]{1,2,0:T(8,128)(2,1)}, s32[128]{0:T(128)S(1)}, /*index=5*...) while((s32[]{:T(128)}, f32[16,128,256]{2,1,0:T(8,128)}, ...), condition=%wide.region_6.7_spmd, body=%wide.region_4.6_spmd.sunk | while | flops 67896424 | bytes 6033887 | solution.py:59
  369.7 2.2 gather_fusion.1
  373.2 3.3 scatter_fusion.1
  377.3 2.2 gather_fusion.1
  380.9 3.4 scatter_fusion.1
  385.0 2.2 gather_fusion.1
  388.6 3.3 scatter_fusion.1
  396.2 3.3 scatter_fusion.1
  403.8 3.3 scatter_fusion.1
  411.4 3.3 scatter_fusion.1
  419.1 3.3 scatter_fusion.1
  426.6 3.3 scatter_fusion.1
  434.2 3.3 scatter_fusion.1
  441.8 3.3 scatter_fusion.1
  449.5 3.3 scatter_fusion.1
  457.0 3.3 scatter_fusion.1
  464.6 3.3 scatter_fusion.1
  472.3 3.3 scatter_fusion.1
  479.9 3.3 scatter_fusion.1
  487.5 3.3 scatter_fusion.1
  490.8 2.7 convert_element_type.62
  493.6 97.8 %psum.15 = f32[256]{0:T(256)} all-reduce(f32[256]{0:T(256)S(1)} %get-tuple-element.297), channel_id=1, replica_groups=mesh['row'=16,'col'=32] {'row','col'}, use_global_device_ids=true, to_apply=%region_10.11 | all-reduce | flops 256 | bytes 2048 | tf_op jit(solution)/shard_map/psum | solution.py:93
  591.4 113.3 %reduce-scatter.5.cloned.1.call-done = bf16[128,256]{1,0:T(8,128)(2,1)} async-done(((bf16[2048,256]{1,0:T(8,128)(2,1)}), bf16[128,256]{1,0:T(8,128)(2,1)}) %reduce-scatter.5.cloned.1.call-update) | async-done | bytes 65552 | tf_op jit(solution)/shard_map/reduce_scatter | solution.py:85
  708.1 273.0 %all-reduce.2.cloned.1.call-done = f32[256,256]{0,1:T(8,128)} async-done(((f32[256,256]{0,1:T(8,128)}), f32[256,256]{0,1:T(8,128)}) %all-reduce.2.cloned.1.call-update) | async-done | bytes 262160 | tf_op jit(solution)/shard_map/psum | solution.py:93
  (184 shorter events, 117.2 us)
Async XLA Ops:
  7.2 0.9 copy-start
  7.2 49.6 %copy-start.3 = (s32[1,1,128]{2,1,0:T(1,128)S(1)}, s32[1,1,128]{2,1,0:T(1,128)}, u32[]{:S(2)}) copy-start(s32[1,1,128]{2,1,0:T(1,128)} %param.16) | copy-start | bytes 1540
  7.2 49.6 %copy-start.4 = (s32[1,1,128]{2,1,0:T(1,128)S(1)}, s32[1,1,128]{2,1,0:T(1,128)}, u32[]{:S(2)}) copy-start(s32[1,1,128]{2,1,0:T(1,128)} %param.17) | copy-start | bytes 1540
  10.2 44.2 %all-to-all-start = ((bf16[16,128,256]{2,1,0:T(8,128)(2,1)}), bf16[16,128,256]{2,1,0:T(8,128)(2,1)S(1)}, u32[]{:S(2)}, u32[]{:S(2)}) async-start(bf16[16,128,256]{2,1,0:T(8,128)(2,1)} %stack.2), calls=%async_computation | async-start | bytes 2097152 | tf_op jit(solution)/shard_map/all_to_all | solution.py:12
  23.8 260.1 %reduce-scatter.3.cloned.1.call-start = ((), (), s32[]{:S(2)}) async-start(), calls=%async_computation.3 | async-start | bytes 2162688 | tf_op jit(solution)/shard_map/reduce_scatter | solution.py:76
  153.2 130.6 %copy-start.2 = (bf16[128,256]{1,0:T(8,128)(2,1)S(1)}, bf16[128,256]{1,0:T(8,128)(2,1)}, u32[]{:S(2)}) copy-start(bf16[128,256]{1,0:T(8,128)(2,1)} %param.15) | copy-start | bytes 196612
  153.2 130.6 %copy-start.5 = (f32[256]{0:T(256)S(1)}, f32[256]{0:T(256)}, u32[]{:S(2)}) copy-start(f32[256]{0:T(256)} %param.14) | copy-start | bytes 3076
  157.1 210.3 %all-gather.2.cloned.1.call-start = ((), (), s32[]{:S(2)}) async-start(), calls=%async_computation.4 | async-start | bytes 2162688 | tf_op jit(solution)/shard_map/all_gather | solution.py:82
  285.4 419.2 %reduce-scatter.5.cloned.1.call-start = ((), (), s32[]{:S(2)}) async-start(), calls=%async_computation.5 | async-start | bytes 1114112 | tf_op jit(solution)/shard_map/reduce_scatter | solution.py:85
  490.8 213.9 %copy-start.1 = (bf16[128,256]{1,0:T(8,128)(2,1)S(1)}, bf16[128,256]{1,0:T(8,128)(2,1)}, u32[]{:S(2)}) copy-start(bf16[128,256]{1,0:T(8,128)(2,1)} %param.12) | copy-start | bytes 196612
  493.5 487.6 %all-reduce.2.cloned.1.call-start = ((), (), s32[]{:S(2)}) async-start(), calls=%async_computation.6 | async-start | bytes 524288 | tf_op jit(solution)/shard_map/psum | solution.py:93
Sparse Core Ops, SparseCore 0:
  157.2 126.5 reduce-scatter.2
  286.8 80.5 all-gather.1
  493.6 210.9 reduce-scatter.4
  710.8 270.2 all-reduce.1
